TPU v7x, 32 devices: a whole 2x2x4 slice. The times are simulated.
32 devices in a mesh: groups: 2 (over y), row: 4 (over z), col: 4 (over x, core).
Axes of the slice: x: 2, y: 2, z: 4, core: 2. Of those that a mesh axis runs over, the one named last changes fastest.
Arguments:
- seq_feat: bfloat16 [64, 256], P(('groups', 'row', 'col')), parts along dimension 0, may hold values from -6 to 6
- lengths: int32 [4], P('groups'), parts along dimension 0, may hold values from 1 to 24, 32 in all
- embed_weight: bfloat16 [2, 256, 128], replicated, may hold values from -0.375 to 0.375
- norm_gain: float32 [4, 128], replicated, may hold values from 0.1 to 1.9
- conv_weight: bfloat16 [4, 3, 3, 128, 128], replicated, may hold values from -0.1875 to 0.1875
- proj_weight: bfloat16 [4, 128, 128], replicated, may hold values from -0.5 to 0.5
- pair_cotangent: bfloat16 [64, 32, 128], P(('groups', 'row'), 'col'), parts along dimension 0, may hold values from -13 to 13
Outputs:
- pair_output: bfloat16 [64, 32, 128], P(('groups', 'row'), 'col'), parts along dimension 0
- seq_grad: float32 [64, 256], P(('groups', 'row', 'col')), parts along dimension 0
- embed_grad: float32 [4, 256, 128], P('groups'), parts along dimension 0
- gain_grad: float32 [8, 128], P('groups'), parts along dimension 0
- conv_grad: float32 [8, 3, 3, 128, 128], P('groups'), parts along dimension 0
- proj_grad: float32 [8, 128, 128], P('groups'), parts along dimension 0
There are 2 independent parts, one for each index of `groups`. A program takes and returns all parts, laid end to end along the dimension named above; an argument that names none is the same for every part. Nothing has to cross between parts.
Inputs may be any that keep to these rules, and one draw needn't show every extreme that they name: lengths[0] residues are real; those at and after index lengths[0] are padding; the two entries sum to 32.
All inputs are finite; a program needn't handle non-finite values.
Results may differ from a plain program's by a relative error of at most 0.014.
Values may be sent and summed in bfloat16 or wider, within the bound.
No kernel may reach another device: no remote copies, remote signals or barrier semaphores. Data moves between devices by JAX's collectives and lax.ppermute only.
A program may use at most 64 MiB of HBM per device.

v0:
```python
import math
import jax
import jax.numpy as jnp
from jax import lax
from jax.sharding import PartitionSpec as P

LAYERS = 4
eps = 1e-05


def with_halo(x, sides, width):
    for axis, dim in sides:
        count, length = (lax.axis_size(axis), x.shape[dim])
        up = [(i, (i + 1) % count) for i in range(count - 1)]
        down = [(j, i) for i, j in up]
        last = lax.slice_in_dim(x, length - width, length, axis=dim)
        first = lax.slice_in_dim(x, 0, width, axis=dim)
        before = lax.ppermute(last, axis, up)
        after = lax.ppermute(first, axis, down)
        x = jnp.concatenate([before, x, after], axis=dim)
    return x


def elu_slope(values):
    return jnp.where(values > 0, 1.0, jnp.exp(jnp.minimum(values, 0.0)))


def normalize(stream, gain_row):
    average = jnp.mean(stream, axis=-1, keepdims=True)
    centred = stream - average
    variance = jnp.mean(centred * centred, axis=-1, keepdims=True)
    inv_std = lax.rsqrt(variance + eps)
    normalized = centred * inv_std
    return (normalized, inv_std, normalized * gain_row)


def conv_forward(padded, weight, spacing, height, width):
    channels = padded.shape[-1]
    summed = jnp.zeros((height * width, weight.shape[-1]), jnp.float32)
    for tap_row in range(3):
        for tap_col in range(3):
            window = padded[
                tap_row * spacing : tap_row * spacing + height,
                tap_col * spacing : tap_col * spacing + width,
                :,
            ]
            summed = summed + jnp.dot(
                window.reshape(height * width, channels),
                weight[tap_row, tap_col],
                preferred_element_type=jnp.float32,
            )
    return summed.reshape(height, width, -1)


def conv_backward(padded, weight, spacing, height, width):
    channels = padded.shape[-1]
    summed = jnp.zeros((height * width, weight.shape[-2]), jnp.float32)
    for tap_row in range(3):
        for tap_col in range(3):
            start_row = (2 - tap_row) * spacing
            start_col = (2 - tap_col) * spacing
            window = padded[start_row : start_row + height, start_col : start_col + width, :]
            summed = summed + jnp.dot(
                window.reshape(height * width, channels),
                weight[tap_row, tap_col].T,
                preferred_element_type=jnp.float32,
            )
    return summed.reshape(height, width, -1)


def conv_weight_grad(padded, grad_tile, spacing, height, width):
    channels = padded.shape[-1]
    flat_grad = grad_tile.reshape(height * width, -1)
    terms = []
    for tap_row in range(3):
        row_terms = []
        for tap_col in range(3):
            window = padded[
                tap_row * spacing : tap_row * spacing + height,
                tap_col * spacing : tap_col * spacing + width,
                :,
            ]
            row_terms.append(
                lax.dot_general(
                    window.reshape(height * width, channels),
                    flat_grad,
                    (((0,), (0,)), ((), ())),
                    preferred_element_type=jnp.float32,
                )
            )
        terms.append(jnp.stack(row_terms))
    return jnp.stack(terms)


def body(seq_feat, lengths, embed_weight, norm_gain, conv_weight, proj_weight, pair_cotangent):
    tile_rows = pair_cotangent.shape[0]
    tile_cols = pair_cotangent.shape[1]
    channels = pair_cotangent.shape[2]
    residues = tile_rows * lax.axis_size("row")
    row_start = lax.axis_index("row") * tile_rows
    col_start = lax.axis_index("col") * tile_cols
    row_live = (row_start + jnp.arange(tile_rows, dtype=jnp.int32) < lengths[0]).astype(jnp.float32)
    col_live = (col_start + jnp.arange(tile_cols, dtype=jnp.int32) < lengths[0]).astype(jnp.float32)
    live_mask = row_live[:, None, None] * col_live[None, :, None]
    gathered = lax.all_gather(seq_feat, ("row", "col"), axis=0, tiled=True)
    row_part = lax.dynamic_slice_in_dim(gathered, row_start, tile_rows, 0)
    col_part = lax.dynamic_slice_in_dim(gathered, col_start, tile_cols, 0)
    row_emb = jnp.dot(row_part, embed_weight[0], preferred_element_type=jnp.float32).astype(
        jnp.bfloat16
    )
    col_emb = jnp.dot(col_part, embed_weight[1], preferred_element_type=jnp.float32).astype(
        jnp.bfloat16
    )
    stream = live_mask * (
        row_emb.astype(jnp.float32)[:, None, :] + col_emb.astype(jnp.float32)[None, :, :]
    )
    stored = []
    for layer_number in range(LAYERS):
        spacing = 2**layer_number
        normalized, inv_std, scaled = normalize(stream, norm_gain[layer_number])
        squashed = (live_mask * jax.nn.elu(scaled)).astype(jnp.bfloat16)
        padded = with_halo(squashed, (("row", 0), ("col", 1)), spacing)
        convolved = conv_forward(padded, conv_weight[layer_number], spacing, tile_rows, tile_cols)
        excited = jax.nn.elu(convolved).astype(jnp.bfloat16)
        update = jnp.dot(
            excited.reshape(-1, channels),
            proj_weight[layer_number],
            preferred_element_type=jnp.float32,
        ).reshape(tile_rows, tile_cols, channels)
        stored.append((stream, padded, convolved, excited))
        stream = stream + live_mask * update
    pair_output = stream.astype(jnp.bfloat16)
    grad_scale = 1.0 / residues
    back_grad = pair_cotangent.astype(jnp.float32)
    gain_terms = [None] * LAYERS
    conv_terms = [None] * LAYERS
    proj_terms = [None] * LAYERS
    for layer_number in reversed(range(LAYERS)):
        spacing = 2**layer_number
        old_stream, padded, convolved, excited = stored[layer_number]
        masked = (live_mask * back_grad).astype(jnp.bfloat16)
        flat_masked = masked.reshape(-1, channels)
        proj_term = (
            lax.dot_general(
                excited.reshape(-1, channels),
                flat_masked,
                (((0,), (0,)), ((), ())),
                preferred_element_type=jnp.float32,
            )
            * grad_scale
        )
        d_excited = jnp.dot(
            flat_masked, proj_weight[layer_number].T, preferred_element_type=jnp.float32
        ).reshape(tile_rows, tile_cols, channels)
        d_pre = (d_excited * elu_slope(convolved)).astype(jnp.bfloat16)
        conv_term = conv_weight_grad(padded, d_pre, spacing, tile_rows, tile_cols) * grad_scale
        d_padded = with_halo(d_pre, (("row", 0), ("col", 1)), spacing)
        d_squashed = conv_backward(
            d_padded, conv_weight[layer_number], spacing, tile_rows, tile_cols
        )
        normalized, inv_std, scaled = normalize(old_stream, norm_gain[layer_number])
        d_scaled = live_mask * d_squashed * elu_slope(scaled)
        gain_term = jnp.sum(d_scaled * normalized, axis=(0, 1)) * grad_scale
        d_norm = d_scaled * norm_gain[layer_number]
        back_grad = back_grad + inv_std * (
            d_norm
            - jnp.mean(d_norm, axis=-1, keepdims=True)
            - normalized * jnp.mean(d_norm * normalized, axis=-1, keepdims=True)
        )
        gain_terms[layer_number] = gain_term
        conv_terms[layer_number] = conv_term
        proj_terms[layer_number] = proj_term
    final_masked = live_mask * back_grad
    row_totals = jnp.sum(final_masked, axis=1)
    col_totals = jnp.sum(final_masked, axis=0)
    d_row = lax.psum_scatter(row_totals, "col", scatter_dimension=0, tiled=True).astype(
        jnp.bfloat16
    )
    spread_cols = lax.dynamic_update_slice_in_dim(
        jnp.zeros((residues, channels), jnp.float32), col_totals, col_start, 0
    )
    d_col = lax.psum_scatter(spread_cols, ("row", "col"), scatter_dimension=0, tiled=True).astype(
        jnp.bfloat16
    )
    seq_grad = (
        jnp.dot(d_row, embed_weight[0].T, preferred_element_type=jnp.float32)
        + jnp.dot(d_col, embed_weight[1].T, preferred_element_type=jnp.float32)
    ) / math.sqrt(residues)
    embed_term = (
        jnp.stack(
            [
                lax.dot_general(
                    seq_feat, d_row, (((0,), (0,)), ((), ())), preferred_element_type=jnp.float32
                ),
                lax.dot_general(
                    seq_feat, d_col, (((0,), (0,)), ((), ())), preferred_element_type=jnp.float32
                ),
            ]
        )
        * grad_scale
    )
    gain_grad = jnp.stack(gain_terms)
    conv_grad = jnp.stack(conv_terms)
    proj_grad = jnp.stack(proj_terms)
    gain_grad, conv_grad, proj_grad, embed_grad = lax.psum(
        (gain_grad, conv_grad, proj_grad, embed_term), ("row", "col")
    )
    return (pair_output, seq_grad, embed_grad, gain_grad, conv_grad, proj_grad)


def solution(mesh):
    placed = (
        P(("groups", "row", "col"), None),
        P("groups"),
        P(),
        P(),
        P(),
        P(),
        P(("groups", "row"), "col", None),
    )
    return jax.shard_map(
        body,
        mesh=mesh,
        in_specs=placed,
        out_specs=(
            P(("groups", "row"), "col", None),
            P(("groups", "row", "col"), None),
            P("groups", None, None),
            P("groups", None),
            P("groups", None, None, None, None),
            P("groups", None, None),
        ),
        check_vma=False,
    )
```

profile of v0, /device:TPU:0, one launch (start us, length us, event | category | flops | bytes accessed | tf_op | source)
XLA Modules:
  0.0 350.0 jit_solution(10148906690786767600)
XLA Ops:
  8.8 23.3 %all-gather = bf16[16,2,256]{2,1,0:T(2,128)(2,1)S(1)} all-gather(bf16[1,2,256]{2,1,0:T(2,128)(2,1)} %bitcast.781), channel_id=1, replica_groups=mesh['groups'=2,'row'=4,'col'=4] {'row','col'}, dimensions={0}, use_global_device_ids=true | all-gather | bytes 17408 | tf_op jit(solution)/shard_map/all_gather | solution.py:105
  35.9 1.3 collective-permute-start.1
  37.2 1.3 slice_bitcast_fusion
  38.5 2.9 collective-permute-done.1
  42.7 1.3 collective-permute-start.3
  44.1 1.6 collective-permute-done.3
  47.4 2.4 collective-permute-start.4
  49.7 1.3 collective-permute-start.5
  53.9 1.3 collective-permute-done.5
  55.3 2.6 collective-permute-start.6
  57.9 1.3 collective-permute-start.7
  59.3 2.4 collective-permute-done.7
  63.3 3.9 %collective-permute-start.8 = (bf16[4,8,128]{2,1,0:T(8,128)(2,1)S(1)}, bf16[4,8,128]{2,1,0:T(8,128)(2,1)S(1)}, u32[]{:S(2)}, u32[]{:S(2)}) collective-permute-start(bf16[4,8,128]{2,1,0:T(8,128)(2,1)S(1)} %get-tuple-element.67), channel_id=1, source_target_pairs={{0,4},{4,8},{8,12},{1,5},{5,9},{9,13},{2,6},{6,10},{10,14},{3,7},{... | collective-permute-start | bytes 24584 | tf_op jit(solution)/shard_map/ppermute | solution.py:18
  67.2 1.3 collective-permute-start.9
  68.6 4.1 %collective-permute-done.9 = bf16[4,8,128]{2,1,0:T(8,128)(2,1)S(1)} collective-permute-done((bf16[4,8,128]{2,1,0:T(8,128)(2,1)S(1)}, bf16[4,8,128]{2,1,0:T(8,128)(2,1)S(1)}, u32[]{:S(2)}, u32[]{:S(2)}) %collective-permute-start.9) | collective-permute-done | bytes 8224 | tf_op jit(solution)/shard_map/ppermute | solution.py:19
  72.8 2.9 collective-permute-start.10
  75.6 1.3 collective-permute-start.11
  77.2 2.5 collective-permute-done.11
  81.0 1.3 collective-permute-start.13
  82.3 4.5 %collective-permute-start.12 = (bf16[8,8,128]{2,1,0:T(8,128)(2,1)S(1)}, bf16[8,8,128]{2,1,0:T(8,128)(2,1)S(1)}, u32[]{:S(2)}, u32[]{:S(2)}) collective-permute-start(bf16[8,8,128]{2,1,0:T(8,128)(2,1)S(1)} %fusion.106), channel_id=1, source_target_pairs={{0,4},{4,8},{8,12},{1,5},{5,9},{9,13},{2,6},{6,10},{10,14},{3,7},{... | collective-permute-start | bytes 49160 | tf_op jit(solution)/shard_map/ppermute | solution.py:18
  87.0 1.3 collective-permute-done.12
  89.6 3.9 %collective-permute-start.14 = (bf16[24,8,128]{2,1,0:T(8,128)(2,1)S(1)}, bf16[24,8,128]{2,1,0:T(8,128)(2,1)S(1)}, u32[]{:S(2)}, u32[]{:S(2)}) collective-permute-start(bf16[24,8,128]{2,1,0:T(8,128)(2,1)S(1)} %pad_maximum_fusion.3), channel_id=1, source_target_pairs={{0,1},{1,2},{2,3},{4,5},{5,6},{6,7},{8,9},{9,10},{10,11},{12,13},{... | collective-permute-start | bytes 147464 | tf_op jit(solution)/shard_map/ppermute | solution.py:18
  95.1 1.3 collective-permute-start.17
  96.4 4.5 %collective-permute-start.16 = (bf16[8,8,128]{2,1,0:T(8,128)(2,1)S(1)}, bf16[8,8,128]{2,1,0:T(8,128)(2,1)S(1)}, u32[]{:S(2)}, u32[]{:S(2)}) collective-permute-start(bf16[8,8,128]{2,1,0:T(8,128)(2,1)S(1)} %fusion.50), channel_id=1, source_target_pairs={{0,4},{4,8},{8,12},{1,5},{5,9},{9,13},{2,6},{6,10},{10,14},{3,7},{... | collective-permute-start | bytes 49160 | tf_op jit(solution)/shard_map/ppermute | solution.py:18
  103.4 3.6 %collective-permute-start.19 = (bf16[24,8,128]{2,1,0:T(8,128)(2,1)S(1)}, bf16[24,8,128]{2,1,0:T(8,128)(2,1)S(1)}, u32[]{:S(2)}, u32[]{:S(2)}) collective-permute-start(bf16[24,8,128]{2,1,0:T(8,128)(2,1)S(1)} %pad_maximum_fusion.4), channel_id=1, source_target_pairs={{0,1},{1,2},{2,3},{4,5},{5,6},{6,7},{8,9},{9,10},{10,11},{12,13},{... | collective-permute-start | bytes 147464 | tf_op jit(solution)/shard_map/ppermute | solution.py:18
  107.1 1.3 collective-permute-start.18
  109.0 3.4 collective-permute-done.18
  113.7 3.9 %collective-permute-start.20 = (bf16[4,8,128]{2,1,0:T(8,128)(2,1)S(1)}, bf16[4,8,128]{2,1,0:T(8,128)(2,1)S(1)}, u32[]{:S(2)}, u32[]{:S(2)}) collective-permute-start(bf16[4,8,128]{2,1,0:T(8,128)(2,1)S(1)} %get-tuple-element.65), channel_id=1, source_target_pairs={{0,4},{4,8},{8,12},{1,5},{5,9},{9,13},{2,6},{6,10},{10,14},{3,7},{... | collective-permute-start | bytes 24584 | tf_op jit(solution)/shard_map/ppermute | solution.py:18
  117.7 1.3 collective-permute-start.21
  121.1 2.1 collective-permute-done.21
  123.2 1.3 collective-permute-start.22
  124.5 3.9 %collective-permute-start.23 = (bf16[16,4,128]{2,1,0:T(4,128)(2,1)S(1)}, bf16[16,4,128]{2,1,0:T(4,128)(2,1)S(1)}, u32[]{:S(2)}, u32[]{:S(2)}) collective-permute-start(bf16[16,4,128]{2,1,0:T(4,128)(2,1)S(1)} %get-tuple-element.42), channel_id=1, source_target_pairs={{0,1},{1,2},{2,3},{4,5},{5,6},{6,7},{8,9},{9,10},{10,11},{12,13},{... | collective-permute-start | bytes 49160 | tf_op jit(solution)/shard_map/ppermute | solution.py:18
  132.1 3.3 collective-permute-start.24
  135.4 1.3 collective-permute-start.25
  137.5 3.4 collective-permute-done.25
  140.9 1.3 collective-permute-start.26
  142.2 3.0 collective-permute-start.27
  149.5 3.3 collective-permute-start.28
  152.8 1.3 collective-permute-start.29
  154.6 1.6 pad_maximum_fusion
  156.9 1.3 collective-permute-done.29
  158.3 1.3 collective-permute-start.30
  159.6 4.6 %collective-permute-start.31 = (bf16[10,1,128]{2,1,0:T(2,128)(2,1)S(1)}, bf16[10,1,128]{2,1,0:T(2,128)(2,1)S(1)}, u32[]{:S(2)}, u32[]{:S(2)}) collective-permute-start(bf16[10,1,128]{2,1,0:T(2,128)(2,1)S(1)} %get-tuple-element.56), channel_id=1, source_target_pairs={{0,1},{1,2},{2,3},{4,5},{5,6},{6,7},{8,9},{9,10},{10,11},{12,13},{... | collective-permute-start | bytes 7688 | tf_op jit(solution)/shard_map/ppermute | solution.py:18
  166.7 9.7 %all-reduce = bf16[8,128]{1,0:T(8,128)(2,1)S(1)} all-reduce(f32[8,128]{1,0:T(8,128)S(1)} %get-tuple-element.31), channel_id=2, replica_groups=mesh['groups'=2,'row'=4,'col'=4] {'col'}, use_global_device_ids=true, to_apply=%region_17.18.clone | all-reduce | flops 1024 | bytes 6144
  176.4 59.6 %all-reduce.2 = (bf16[32,128]{1,0:T(8,128)(2,1)S(1)}, f32[4,128]{1,0:T(4,128)}) all-reduce(f32[32,128]{1,0:T(8,128)S(1)} %constant_dynamic-update-slice_fusion, f32[4,128]{1,0:T(4,128)S(1)} %pad_maximum_fusion.48), channel_id=3, replica_groups=mesh['groups'=2,'row'=4,'col'=4] {'row','col'}, use_global_device_ids=true, to_apply=%region_19.20.clone | all-reduce | flops 4608 | bytes 28672
  238.9 98.4 %all-reduce.6.cloned.1.call-done = (f32[2,256,128]{1,2,0:T(8,128)}, f32[4,3,3,128,128]{4,3,2,1,0:T(8,128)}, f32[4,128,128]{2,1,0:T(8,128)}) async-done(((f32[2,256,128]{1,2,0:T(8,128)}, f32[4,3,3,128,128]{4,3,2,1,0:T(8,128)}, f32[4,128,128]{2,1,0:T(8,128)}), (f32[2,256,128]{1,2,0:T(8,128)}, f32[4,3,3,128,128]{4,3,2,1,0:T(8,128)}, f32[4,128,128]{2,1,0:T(8,128)})) %all-reduce.6.cloned.1.call-update) | async-done | bytes 2883600 | tf_op jit(solution)/shard_map/psum | solution.py:205
  337.3 1.8 copy.14
  339.1 3.4 copy.19
  (256 shorter events, 38.6 us)
Async XLA Ops:
  7.2 44.0 %copy-start.6 = (u32[32]{0:T(128)S(1)}, u32[32]{0:T(128)}, u32[]{:S(2)}) copy-start(u32[32]{0:T(128)} %constant.72) | copy-start | bytes 388
  7.2 44.6 %copy-start.5 = (u32[32]{0:T(128)S(1)}, u32[32]{0:T(128)}, u32[]{:S(2)}) copy-start(u32[32]{0:T(128)} %constant.68) | copy-start | bytes 388
  7.2 39.7 %copy-start.1 = (bf16[4,128,128]{2,1,0:T(8,128)(2,1)S(1)}, bf16[4,128,128]{2,1,0:T(8,128)(2,1)}, u32[]{:S(2)}) copy-start(bf16[4,128,128]{2,1,0:T(8,128)(2,1)} %param.12) | copy-start | bytes 393220
  7.2 330.1 %all-reduce.6.cloned.1.call-start = ((), (), s32[]{:S(2)}) async-start(), calls=%async_computation | async-start | bytes 5767168 | tf_op jit(solution)/shard_map/psum | solution.py:205
  34.6 3.9 %collective-permute-start = (bf16[1,8,128]{2,1,0:T(8,128)(2,1)S(1)}, bf16[1,8,128]{2,1,0:T(8,128)(2,1)S(1)}, u32[]{:S(2)}, u32[]{:S(2)}) collective-permute-start(bf16[1,8,128]{2,1,0:T(8,128)(2,1)S(1)} %get-tuple-element.71), channel_id=1, source_target_pairs={{0,4},{4,8},{8,12},{1,5},{5,9},{9,13},{2,6},{6,10},{10,14},{3,7},{... | collective-permute-start | bytes 6152 | tf_op jit(solution)/shard_map/ppermute | solution.py:18
  35.9 5.5 %collective-permute-start.1 = (bf16[1,8,128]{2,1,0:T(8,128)(2,1)S(1)}, bf16[1,8,128]{2,1,0:T(8,128)(2,1)S(1)}, u32[]{:S(2)}, u32[]{:S(2)}) collective-permute-start(bf16[1,8,128]{2,1,0:T(8,128)(2,1)S(1)} %get-tuple-element.72), channel_id=1, source_target_pairs={{4,0},{8,4},{12,8},{5,1},{9,5},{13,9},{6,2},{10,6},{14,10},{7,3},{... | collective-permute-start | bytes 6152 | tf_op jit(solution)/shard_map/ppermute | solution.py:19
  41.4 2.7 collective-permute-start.2
  42.7 3.1 collective-permute-start.3
  46.7 48.2 %copy-start.3 = (bf16[8,8,128]{2,1,0:T(8,128)(2,1)S(1)}, bf16[8,8,128]{2,1,0:T(8,128)(2,1)}, u32[]{:S(2)}) copy-start(bf16[8,8,128]{2,1,0:T(8,128)(2,1)} %param.13) | copy-start | bytes 49156
  47.4 6.6 %collective-permute-start.4 = (bf16[2,8,128]{2,1,0:T(8,128)(2,1)S(1)}, bf16[2,8,128]{2,1,0:T(8,128)(2,1)S(1)}, u32[]{:S(2)}, u32[]{:S(2)}) collective-permute-start(bf16[2,8,128]{2,1,0:T(8,128)(2,1)S(1)} %get-tuple-element.69), channel_id=1, source_target_pairs={{0,4},{4,8},{8,12},{1,5},{5,9},{9,13},{2,6},{6,10},{10,14},{3,7},{... | collective-permute-start | bytes 12296 | tf_op jit(solution)/shard_map/ppermute | solution.py:18
  49.7 5.5 %collective-permute-start.5 = (bf16[2,8,128]{2,1,0:T(8,128)(2,1)S(1)}, bf16[2,8,128]{2,1,0:T(8,128)(2,1)S(1)}, u32[]{:S(2)}, u32[]{:S(2)}) collective-permute-start(bf16[2,8,128]{2,1,0:T(8,128)(2,1)S(1)} %get-tuple-element.70), channel_id=1, source_target_pairs={{4,0},{8,4},{12,8},{5,1},{9,5},{13,9},{6,2},{10,6},{14,10},{7,3},{... | collective-permute-start | bytes 12296 | tf_op jit(solution)/shard_map/ppermute | solution.py:19
  55.3 4.1 %collective-permute-start.6 = (bf16[12,2,128]{2,1,0:T(2,128)(2,1)S(1)}, bf16[12,2,128]{2,1,0:T(2,128)(2,1)S(1)}, u32[]{:S(2)}, u32[]{:S(2)}) collective-permute-start(bf16[12,2,128]{2,1,0:T(2,128)(2,1)S(1)} %get-tuple-element.51), channel_id=1, source_target_pairs={{0,1},{1,2},{2,3},{4,5},{5,6},{6,7},{8,9},{9,10},{10,11},{12,13},{... | collective-permute-start | bytes 18440 | tf_op jit(solution)/shard_map/ppermute | solution.py:18
  57.9 3.8 %collective-permute-start.7 = (bf16[12,2,128]{2,1,0:T(2,128)(2,1)S(1)}, bf16[12,2,128]{2,1,0:T(2,128)(2,1)S(1)}, u32[]{:S(2)}, u32[]{:S(2)}) collective-permute-start(bf16[12,2,128]{2,1,0:T(2,128)(2,1)S(1)} %get-tuple-element.52), channel_id=1, source_target_pairs={{1,0},{2,1},{3,2},{5,4},{6,5},{7,6},{9,8},{10,9},{11,10},{13,12},{... | collective-permute-start | bytes 18440 | tf_op jit(solution)/shard_map/ppermute | solution.py:19
  63.3 5.3 %collective-permute-start.8 = (bf16[4,8,128]{2,1,0:T(8,128)(2,1)S(1)}, bf16[4,8,128]{2,1,0:T(8,128)(2,1)S(1)}, u32[]{:S(2)}, u32[]{:S(2)}) collective-permute-start(bf16[4,8,128]{2,1,0:T(8,128)(2,1)S(1)} %get-tuple-element.67), channel_id=1, source_target_pairs={{0,4},{4,8},{8,12},{1,5},{5,9},{9,13},{2,6},{6,10},{10,14},{3,7},{... | collective-permute-start | bytes 24584 | tf_op jit(solution)/shard_map/ppermute | solution.py:18
  67.2 5.5 %collective-permute-start.9 = (bf16[4,8,128]{2,1,0:T(8,128)(2,1)S(1)}, bf16[4,8,128]{2,1,0:T(8,128)(2,1)S(1)}, u32[]{:S(2)}, u32[]{:S(2)}) collective-permute-start(bf16[4,8,128]{2,1,0:T(8,128)(2,1)S(1)} %get-tuple-element.68), channel_id=1, source_target_pairs={{4,0},{8,4},{12,8},{5,1},{9,5},{13,9},{6,2},{10,6},{14,10},{7,3},{... | collective-permute-start | bytes 24584 | tf_op jit(solution)/shard_map/ppermute | solution.py:19
  72.8 7.2 %collective-permute-start.10 = (bf16[16,4,128]{2,1,0:T(4,128)(2,1)S(1)}, bf16[16,4,128]{2,1,0:T(4,128)(2,1)S(1)}, u32[]{:S(2)}, u32[]{:S(2)}) collective-permute-start(bf16[16,4,128]{2,1,0:T(4,128)(2,1)S(1)} %get-tuple-element.43), channel_id=1, source_target_pairs={{0,1},{1,2},{2,3},{4,5},{5,6},{6,7},{8,9},{9,10},{10,11},{12,13},{... | collective-permute-start | bytes 49160 | tf_op jit(solution)/shard_map/ppermute | solution.py:18
  75.6 4.1 %collective-permute-start.11 = (bf16[16,4,128]{2,1,0:T(4,128)(2,1)S(1)}, bf16[16,4,128]{2,1,0:T(4,128)(2,1)S(1)}, u32[]{:S(2)}, u32[]{:S(2)}) collective-permute-start(bf16[16,4,128]{2,1,0:T(4,128)(2,1)S(1)} %get-tuple-element.44), channel_id=1, source_target_pairs={{1,0},{2,1},{3,2},{5,4},{6,5},{7,6},{9,8},{10,9},{11,10},{13,12},{... | collective-permute-start | bytes 49160 | tf_op jit(solution)/shard_map/ppermute | solution.py:19
  81.0 6.0 %collective-permute-start.13 = (bf16[8,8,128]{2,1,0:T(8,128)(2,1)S(1)}, bf16[8,8,128]{2,1,0:T(8,128)(2,1)S(1)}, u32[]{:S(2)}, u32[]{:S(2)}) collective-permute-start(bf16[8,8,128]{2,1,0:T(8,128)(2,1)S(1)} %fusion.106), channel_id=1, source_target_pairs={{4,0},{8,4},{12,8},{5,1},{9,5},{13,9},{6,2},{10,6},{14,10},{7,3},{... | collective-permute-start | bytes 49160 | tf_op jit(solution)/shard_map/ppermute | solution.py:19
  82.3 6.0 %collective-permute-start.12 = (bf16[8,8,128]{2,1,0:T(8,128)(2,1)S(1)}, bf16[8,8,128]{2,1,0:T(8,128)(2,1)S(1)}, u32[]{:S(2)}, u32[]{:S(2)}) collective-permute-start(bf16[8,8,128]{2,1,0:T(8,128)(2,1)S(1)} %fusion.106), channel_id=1, source_target_pairs={{0,4},{4,8},{8,12},{1,5},{5,9},{9,13},{2,6},{6,10},{10,14},{3,7},{... | collective-permute-start | bytes 49160 | tf_op jit(solution)/shard_map/ppermute | solution.py:18
  88.3 5.4 %collective-permute-start.15 = (bf16[24,8,128]{2,1,0:T(8,128)(2,1)S(1)}, bf16[24,8,128]{2,1,0:T(8,128)(2,1)S(1)}, u32[]{:S(2)}, u32[]{:S(2)}) collective-permute-start(bf16[24,8,128]{2,1,0:T(8,128)(2,1)S(1)} %pad_maximum_fusion.3), channel_id=1, source_target_pairs={{1,0},{2,1},{3,2},{5,4},{6,5},{7,6},{9,8},{10,9},{11,10},{13,12},{... | collective-permute-start | bytes 147464 | tf_op jit(solution)/shard_map/ppermute | solution.py:19
  89.6 4.7 %collective-permute-start.14 = (bf16[24,8,128]{2,1,0:T(8,128)(2,1)S(1)}, bf16[24,8,128]{2,1,0:T(8,128)(2,1)S(1)}, u32[]{:S(2)}, u32[]{:S(2)}) collective-permute-start(bf16[24,8,128]{2,1,0:T(8,128)(2,1)S(1)} %pad_maximum_fusion.3), channel_id=1, source_target_pairs={{0,1},{1,2},{2,3},{4,5},{5,6},{6,7},{8,9},{9,10},{10,11},{12,13},{... | collective-permute-start | bytes 147464 | tf_op jit(solution)/shard_map/ppermute | solution.py:18
  95.1 8.3 %collective-permute-start.17 = (bf16[8,8,128]{2,1,0:T(8,128)(2,1)S(1)}, bf16[8,8,128]{2,1,0:T(8,128)(2,1)S(1)}, u32[]{:S(2)}, u32[]{:S(2)}) collective-permute-start(bf16[8,8,128]{2,1,0:T(8,128)(2,1)S(1)} %fusion.50), channel_id=1, source_target_pairs={{4,0},{8,4},{12,8},{5,1},{9,5},{13,9},{6,2},{10,6},{14,10},{7,3},{... | collective-permute-start | bytes 49160 | tf_op jit(solution)/shard_map/ppermute | solution.py:19
  96.4 7.0 %collective-permute-start.16 = (bf16[8,8,128]{2,1,0:T(8,128)(2,1)S(1)}, bf16[8,8,128]{2,1,0:T(8,128)(2,1)S(1)}, u32[]{:S(2)}, u32[]{:S(2)}) collective-permute-start(bf16[8,8,128]{2,1,0:T(8,128)(2,1)S(1)} %fusion.50), channel_id=1, source_target_pairs={{0,4},{4,8},{8,12},{1,5},{5,9},{9,13},{2,6},{6,10},{10,14},{3,7},{... | collective-permute-start | bytes 49160 | tf_op jit(solution)/shard_map/ppermute | solution.py:18
  103.4 5.2 %collective-permute-start.19 = (bf16[24,8,128]{2,1,0:T(8,128)(2,1)S(1)}, bf16[24,8,128]{2,1,0:T(8,128)(2,1)S(1)}, u32[]{:S(2)}, u32[]{:S(2)}) collective-permute-start(bf16[24,8,128]{2,1,0:T(8,128)(2,1)S(1)} %pad_maximum_fusion.4), channel_id=1, source_target_pairs={{0,1},{1,2},{2,3},{4,5},{5,6},{6,7},{8,9},{9,10},{10,11},{12,13},{... | collective-permute-start | bytes 147464 | tf_op jit(solution)/shard_map/ppermute | solution.py:18
  107.1 5.3 %collective-permute-start.18 = (bf16[24,8,128]{2,1,0:T(8,128)(2,1)S(1)}, bf16[24,8,128]{2,1,0:T(8,128)(2,1)S(1)}, u32[]{:S(2)}, u32[]{:S(2)}) collective-permute-start(bf16[24,8,128]{2,1,0:T(8,128)(2,1)S(1)} %pad_maximum_fusion.4), channel_id=1, source_target_pairs={{1,0},{2,1},{3,2},{5,4},{6,5},{7,6},{9,8},{10,9},{11,10},{13,12},{... | collective-permute-start | bytes 147464 | tf_op jit(solution)/shard_map/ppermute | solution.py:19
  113.7 7.3 %collective-permute-start.20 = (bf16[4,8,128]{2,1,0:T(8,128)(2,1)S(1)}, bf16[4,8,128]{2,1,0:T(8,128)(2,1)S(1)}, u32[]{:S(2)}, u32[]{:S(2)}) collective-permute-start(bf16[4,8,128]{2,1,0:T(8,128)(2,1)S(1)} %get-tuple-element.65), channel_id=1, source_target_pairs={{0,4},{4,8},{8,12},{1,5},{5,9},{9,13},{2,6},{6,10},{10,14},{3,7},{... | collective-permute-start | bytes 24584 | tf_op jit(solution)/shard_map/ppermute | solution.py:18
  117.7 5.5 %collective-permute-start.21 = (bf16[4,8,128]{2,1,0:T(8,128)(2,1)S(1)}, bf16[4,8,128]{2,1,0:T(8,128)(2,1)S(1)}, u32[]{:S(2)}, u32[]{:S(2)}) collective-permute-start(bf16[4,8,128]{2,1,0:T(8,128)(2,1)S(1)} %get-tuple-element.66), channel_id=1, source_target_pairs={{4,0},{8,4},{12,8},{5,1},{9,5},{13,9},{6,2},{10,6},{14,10},{7,3},{... | collective-permute-start | bytes 24584 | tf_op jit(solution)/shard_map/ppermute | solution.py:19
  123.2 6.3 %collective-permute-start.22 = (bf16[16,4,128]{2,1,0:T(4,128)(2,1)S(1)}, bf16[16,4,128]{2,1,0:T(4,128)(2,1)S(1)}, u32[]{:S(2)}, u32[]{:S(2)}) collective-permute-start(bf16[16,4,128]{2,1,0:T(4,128)(2,1)S(1)} %get-tuple-element.41), channel_id=1, source_target_pairs={{1,0},{2,1},{3,2},{5,4},{6,5},{7,6},{9,8},{10,9},{11,10},{13,12},{... | collective-permute-start | bytes 49160 | tf_op jit(solution)/shard_map/ppermute | solution.py:19
  124.5 4.7 %collective-permute-start.23 = (bf16[16,4,128]{2,1,0:T(4,128)(2,1)S(1)}, bf16[16,4,128]{2,1,0:T(4,128)(2,1)S(1)}, u32[]{:S(2)}, u32[]{:S(2)}) collective-permute-start(bf16[16,4,128]{2,1,0:T(4,128)(2,1)S(1)} %get-tuple-element.42), channel_id=1, source_target_pairs={{0,1},{1,2},{2,3},{4,5},{5,6},{6,7},{8,9},{9,10},{10,11},{12,13},{... | collective-permute-start | bytes 49160 | tf_op jit(solution)/shard_map/ppermute | solution.py:18
  132.1 5.4 %collective-permute-start.24 = (bf16[2,8,128]{2,1,0:T(8,128)(2,1)S(1)}, bf16[2,8,128]{2,1,0:T(8,128)(2,1)S(1)}, u32[]{:S(2)}, u32[]{:S(2)}) collective-permute-start(bf16[2,8,128]{2,1,0:T(8,128)(2,1)S(1)} %get-tuple-element.63), channel_id=1, source_target_pairs={{0,4},{4,8},{8,12},{1,5},{5,9},{9,13},{2,6},{6,10},{10,14},{3,7},{... | collective-permute-start | bytes 12296 | tf_op jit(solution)/shard_map/ppermute | solution.py:18
  135.4 5.5 %collective-permute-start.25 = (bf16[2,8,128]{2,1,0:T(8,128)(2,1)S(1)}, bf16[2,8,128]{2,1,0:T(8,128)(2,1)S(1)}, u32[]{:S(2)}, u32[]{:S(2)}) collective-permute-start(bf16[2,8,128]{2,1,0:T(8,128)(2,1)S(1)} %get-tuple-element.64), channel_id=1, source_target_pairs={{4,0},{8,4},{12,8},{5,1},{9,5},{13,9},{6,2},{10,6},{14,10},{7,3},{... | collective-permute-start | bytes 12296 | tf_op jit(solution)/shard_map/ppermute | solution.py:19
  140.9 4.5 %collective-permute-start.26 = (bf16[12,2,128]{2,1,0:T(2,128)(2,1)S(1)}, bf16[12,2,128]{2,1,0:T(2,128)(2,1)S(1)}, u32[]{:S(2)}, u32[]{:S(2)}) collective-permute-start(bf16[12,2,128]{2,1,0:T(2,128)(2,1)S(1)} %get-tuple-element.47), channel_id=1, source_target_pairs={{1,0},{2,1},{3,2},{5,4},{6,5},{7,6},{9,8},{10,9},{11,10},{13,12},{... | collective-permute-start | bytes 18440 | tf_op jit(solution)/shard_map/ppermute | solution.py:19
  142.2 3.8 %collective-permute-start.27 = (bf16[12,2,128]{2,1,0:T(2,128)(2,1)S(1)}, bf16[12,2,128]{2,1,0:T(2,128)(2,1)S(1)}, u32[]{:S(2)}, u32[]{:S(2)}) collective-permute-start(bf16[12,2,128]{2,1,0:T(2,128)(2,1)S(1)} %get-tuple-element.48), channel_id=1, source_target_pairs={{0,1},{1,2},{2,3},{4,5},{5,6},{6,7},{8,9},{9,10},{10,11},{12,13},{... | collective-permute-start | bytes 18440 | tf_op jit(solution)/shard_map/ppermute | solution.py:18
  149.5 7.4 %collective-permute-start.28 = (bf16[1,8,128]{2,1,0:T(8,128)(2,1)S(1)}, bf16[1,8,128]{2,1,0:T(8,128)(2,1)S(1)}, u32[]{:S(2)}, u32[]{:S(2)}) collective-permute-start(bf16[1,8,128]{2,1,0:T(8,128)(2,1)S(1)} %get-tuple-element.61), channel_id=1, source_target_pairs={{0,4},{4,8},{8,12},{1,5},{5,9},{9,13},{2,6},{6,10},{10,14},{3,7},{... | collective-permute-start | bytes 6152 | tf_op jit(solution)/shard_map/ppermute | solution.py:18
  152.8 5.5 %collective-permute-start.29 = (bf16[1,8,128]{2,1,0:T(8,128)(2,1)S(1)}, bf16[1,8,128]{2,1,0:T(8,128)(2,1)S(1)}, u32[]{:S(2)}, u32[]{:S(2)}) collective-permute-start(bf16[1,8,128]{2,1,0:T(8,128)(2,1)S(1)} %get-tuple-element.62), channel_id=1, source_target_pairs={{4,0},{8,4},{12,8},{5,1},{9,5},{13,9},{6,2},{10,6},{14,10},{7,3},{... | collective-permute-start | bytes 6152 | tf_op jit(solution)/shard_map/ppermute | solution.py:19
  154.6 81.4 %copy-start.4 = (bf16[2,256]{1,0:T(2,128)(2,1)S(1)}, bf16[2,256]{1,0:T(2,128)(2,1)}, u32[]{:S(2)}) copy-start(bf16[2,256]{1,0:T(2,128)(2,1)} %param.7) | copy-start | bytes 3076
  158.3 6.1 %collective-permute-start.30 = (bf16[10,1,128]{2,1,0:T(2,128)(2,1)S(1)}, bf16[10,1,128]{2,1,0:T(2,128)(2,1)S(1)}, u32[]{:S(2)}, u32[]{:S(2)}) collective-permute-start(bf16[10,1,128]{2,1,0:T(2,128)(2,1)S(1)} %get-tuple-element.55), channel_id=1, source_target_pairs={{1,0},{2,1},{3,2},{5,4},{6,5},{7,6},{9,8},{10,9},{11,10},{13,12},{... | collective-permute-start | bytes 7688 | tf_op jit(solution)/shard_map/ppermute | solution.py:19
  159.6 5.4 %collective-permute-start.31 = (bf16[10,1,128]{2,1,0:T(2,128)(2,1)S(1)}, bf16[10,1,128]{2,1,0:T(2,128)(2,1)S(1)}, u32[]{:S(2)}, u32[]{:S(2)}) collective-permute-start(bf16[10,1,128]{2,1,0:T(2,128)(2,1)S(1)} %get-tuple-element.56), channel_id=1, source_target_pairs={{0,1},{1,2},{2,3},{4,5},{5,6},{6,7},{8,9},{9,10},{10,11},{12,13},{... | collective-permute-start | bytes 7688 | tf_op jit(solution)/shard_map/ppermute | solution.py:18
  165.5 72.5 %copy-start = (bf16[2,256,128]{2,1,0:T(8,128)(2,1)S(1)}, bf16[2,256,128]{2,1,0:T(8,128)(2,1)}, u32[]{:S(2)}) copy-start(bf16[2,256,128]{2,1,0:T(8,128)(2,1)} %param.9) | copy-start | bytes 393220
  339.1 3.4 copy-start.2
Sparse Core Ops, SparseCore 0:
  237.4 99.8 all-reduce.5
where the time goes:
time: 351 us; the launch traced here: 350 us
  waiting for transfers between devices  127 us (36%)
  blocking collectives  92.6 us (26%)
  starting transfers between devices  73.6 us (21%)
  matrix products  24.4 us (7%)
  between operations  16.3 us (5%)
  local copies, waits for them, and re-layouts  9.82 us (3%)
  other arithmetic  6.18 us (2%)
    psum x1, waiting for transfers between devices, body(): lax.psum((gain_grad, conv_grad, proj_grad, embed_term), ('row', 'col'))  98.4 us
    unnamed x2, blocking collectives  69.3 us
    ppermute x16, starting transfers between devices, with_halo(): before = lax.ppermute(last, axis, up)  52.9 us
    ppermute x16, waiting for transfers between devices, with_halo(): after = lax.ppermute(first, axis, down)  25 us
    all_gather x1, blocking collectives, body(): gathered = lax.all_gather(seq_feat, ('row', 'col'), axis=0, tiled=True)  23.3 us
    ppermute x16, starting transfers between devices, with_halo(): after = lax.ppermute(first, axis, down)  20.7 us
    dot_general x36, matrix products, conv_weight_grad(): lax.dot_general(window.reshape(height * width, channels), flat_grad, (((0...  7.69 us
    unnamed x20, local copies, waits for them, and re-layouts  7.07 us
  transfers between devices with their start and end apart: 33, of which 16 were waited for; matrix products, arithmetic and copies ran while one was open for 4% of the time, Pallas kernels for 0%

commit v1 on v0

--- a/solution.py
+++ b/solution.py
@@ -202,8 +202,12 @@
     gain_grad = jnp.stack(gain_terms)
     conv_grad = jnp.stack(conv_terms)
     proj_grad = jnp.stack(proj_terms)
-    gain_grad, conv_grad, proj_grad, embed_grad = lax.psum(
-        (gain_grad, conv_grad, proj_grad, embed_term), ("row", "col")
+
+    def trace_spot(in_array):
+        return lax.psum(lax.psum(in_array, "col"), "row")
+
+    gain_grad, conv_grad, proj_grad, embed_grad = trace_spot(
+        (gain_grad, conv_grad, proj_grad, embed_term)
     )
     return (pair_output, seq_grad, embed_grad, gain_grad, conv_grad, proj_grad)
 

time: 351 us -> 428 us (1.22)
  waiting for transfers between devices: 127 us -> 192 us
  blocking collectives: 92.6 us -> 104 us
    psum x1 -> x2, waiting for transfers between devices: 98.4 us -> 164 us  [trace_spot(): return lax.psum(lax.psum(in_array, 'col'), 'row')]
    psum x0 -> x1, blocking collectives: none -> 12.4 us  [trace_spot(): return lax.psum(lax.psum(in_array, 'col'), 'row')]
  transfers between devices with their start and end apart: 33 -> 34, of which waited for: 16 -> 17; matrix products, arithmetic and copies ran while one was open for 4% -> 4% of each run, Pallas kernels for 0% -> 0%
where the time goes in v1:
time: 428 us; the launch traced here: 427 us
  waiting for transfers between devices  192 us (45%)
  blocking collectives  104 us (24%)
  starting transfers between devices  73.7 us (17%)
  matrix products  24.4 us (6%)
  between operations  16.3 us (4%)
  local copies, waits for them, and re-layouts  9.83 us (2%)
  other arithmetic  6.18 us (1%)
    psum x2, waiting for transfers between devices, trace_spot(): return lax.psum(lax.psum(in_array, 'col'), 'row')  164 us
    unnamed x2, blocking collectives  68.3 us
    ppermute x16, starting transfers between devices, with_halo(): before = lax.ppermute(last, axis, up)  52.9 us
    ppermute x16, waiting for transfers between devices, with_halo(): after = lax.ppermute(first, axis, down)  25 us
    all_gather x1, blocking collectives, body(): gathered = lax.all_gather(seq_feat, ('row', 'col'), axis=0, tiled=True)  23.3 us
    ppermute x16, starting transfers between devices, with_halo(): after = lax.ppermute(first, axis, down)  20.7 us
    psum x1, blocking collectives, trace_spot(): return lax.psum(lax.psum(in_array, 'col'), 'row')  12.4 us
  transfers between devices with their start and end apart: 34, of which 17 were waited for; matrix products, arithmetic and copies ran while one was open for 4% of the time, Pallas kernels for 0%

profile of v1, /device:TPU:0, one launch (start us, length us, event | category | flops | bytes accessed | tf_op | source)
XLA Modules:
  0.0 426.8 jit_solution(16562756680698050558)
XLA Ops:
  8.8 23.3 %all-gather = bf16[16,2,256]{2,1,0:T(2,128)(2,1)S(1)} all-gather(bf16[1,2,256]{2,1,0:T(2,128)(2,1)} %bitcast.781), channel_id=1, replica_groups=mesh['groups'=2,'row'=4,'col'=4] {'row','col'}, dimensions={0}, use_global_device_ids=true | all-gather | bytes 17408 | tf_op jit(solution)/shard_map/all_gather | solution.py:105
  35.9 1.3 collective-permute-start.1
  37.2 1.3 slice_bitcast_fusion
  38.5 2.9 collective-permute-done.1
  42.7 1.3 collective-permute-start.3
  44.1 1.6 collective-permute-done.3
  47.4 2.4 collective-permute-start.4
  49.7 1.3 collective-permute-start.5
  53.9 1.3 collective-permute-done.5
  55.3 2.6 collective-permute-start.6
  57.9 1.3 collective-permute-start.7
  59.3 2.4 collective-permute-done.7
  63.3 3.9 collective-permute-start.8
  67.2 1.3 collective-permute-start.9
  68.6 4.1 collective-permute-done.9
  72.8 2.9 collective-permute-start.10
  75.6 1.3 collective-permute-start.11
  77.2 2.5 collective-permute-done.11
  81.0 1.3 collective-permute-start.13
  82.3 4.5 %collective-permute-start.12 = (bf16[8,8,128]{2,1,0:T(8,128)(2,1)S(1)}, bf16[8,8,128]{2,1,0:T(8,128)(2,1)S(1)}, u32[]{:S(2)}, u32[]{:S(2)}) collective-permute-start(bf16[8,8,128]{2,1,0:T(8,128)(2,1)S(1)} %fusion.106), channel_id=1, source_target_pairs={{0,4},{4,8},{8,12},{1,5},{5,9},{9,13},{2,6},{6,10},{10,14},{3,7},{... | collective-permute-start | bytes 49160 | tf_op jit(solution)/shard_map/ppermute | solution.py:18
  87.0 1.3 collective-permute-done.12
  89.6 3.9 collective-permute-start.14
  95.1 1.3 collective-permute-start.17
  96.4 4.5 %collective-permute-start.16 = (bf16[8,8,128]{2,1,0:T(8,128)(2,1)S(1)}, bf16[8,8,128]{2,1,0:T(8,128)(2,1)S(1)}, u32[]{:S(2)}, u32[]{:S(2)}) collective-permute-start(bf16[8,8,128]{2,1,0:T(8,128)(2,1)S(1)} %fusion.50), channel_id=1, source_target_pairs={{0,4},{4,8},{8,12},{1,5},{5,9},{9,13},{2,6},{6,10},{10,14},{3,7},{... | collective-permute-start | bytes 49160 | tf_op jit(solution)/shard_map/ppermute | solution.py:18
  103.4 3.6 collective-permute-start.19
  107.1 1.3 collective-permute-start.18
  109.0 3.4 collective-permute-done.18
  113.7 3.9 collective-permute-start.20
  117.7 1.3 collective-permute-start.21
  121.1 2.1 collective-permute-done.21
  123.2 1.3 collective-permute-start.22
  124.5 3.9 collective-permute-start.23
  132.1 3.3 collective-permute-start.24
  135.4 1.3 collective-permute-start.25
  137.5 3.4 collective-permute-done.25
  140.9 1.3 collective-permute-start.26
  142.2 3.0 collective-permute-start.27
  149.5 3.3 collective-permute-start.28
  154.6 1.6 pad_maximum_fusion
  156.9 1.3 collective-permute-done.29
  159.6 4.6 %collective-permute-start.31 = (bf16[10,1,128]{2,1,0:T(2,128)(2,1)S(1)}, bf16[10,1,128]{2,1,0:T(2,128)(2,1)S(1)}, u32[]{:S(2)}, u32[]{:S(2)}) collective-permute-start(bf16[10,1,128]{2,1,0:T(2,128)(2,1)S(1)} %get-tuple-element.59), channel_id=1, source_target_pairs={{0,1},{1,2},{2,3},{4,5},{5,6},{6,7},{8,9},{9,10},{10,11},{12,13},{... | collective-permute-start | bytes 7688 | tf_op jit(solution)/shard_map/ppermute | solution.py:18
  166.7 62.4 %all-reduce.1 = bf16[32,128]{1,0:T(8,128)(2,1)S(1)} all-reduce(f32[32,128]{1,0:T(8,128)S(1)} %constant_dynamic-update-slice_fusion), channel_id=3, replica_groups=mesh['groups'=2,'row'=4,'col'=4] {'row','col'}, use_global_device_ids=true, to_apply=%region_19.20.clone | all-reduce | flops 4096 | bytes 24576
  229.2 5.8 %all-reduce.2 = (bf16[8,128]{1,0:T(8,128)(2,1)S(1)}, f32[4,128]{1,0:T(4,128)S(1)}) all-reduce(f32[8,128]{1,0:T(8,128)S(1)} %get-tuple-element.31, f32[4,128]{1,0:T(4,128)S(1)} %pad_maximum_fusion.48), channel_id=2, replica_groups=mesh['groups'=2,'row'=4,'col'=4] {'col'}, use_global_device_ids=true, to_apply=%region_17.18.clone | all-reduce | flops 1536 | bytes 10240
  236.3 61.9 %all-reduce.8.cloned.1.call-done = (f32[2,256,128]{1,2,0:T(8,128)}, f32[4,3,3,128,128]{4,3,2,1,0:T(8,128)}, f32[4,128,128]{2,1,0:T(8,128)}) async-done(((f32[2,256,128]{1,2,0:T(8,128)}, f32[4,3,3,128,128]{4,3,2,1,0:T(8,128)}, f32[4,128,128]{2,1,0:T(8,128)}), (f32[2,256,128]{1,2,0:T(8,128)}, f32[4,3,3,128,128]{4,3,2,1,0:T(8,128)}, f32[4,128,128]{2,1,0:T(8,128)})) %all-reduce.8.cloned.1.call-update) | async-done | bytes 2883600 | tf_op jit(solution)/shard_map/psum | solution.py:207
  299.0 12.4 %psum.59 = f32[4,128]{1,0:T(4,128)} all-reduce(f32[4,128]{1,0:T(4,128)S(1)} %get-tuple-element.33), channel_id=1, replica_groups=mesh['groups'=2,'row'=4,'col'=4] {'row'}, use_global_device_ids=true, to_apply=%region_27.28 | all-reduce | flops 512 | bytes 4096 | tf_op jit(solution)/shard_map/psum | solution.py:207
  312.2 101.9 %all-reduce.10.cloned.1.call-done = (f32[2,256,128]{1,2,0:T(8,128)}, f32[4,3,3,128,128]{4,3,2,1,0:T(8,128)}, f32[4,128,128]{2,1,0:T(8,128)}) async-done(((f32[2,256,128]{1,2,0:T(8,128)}, f32[4,3,3,128,128]{4,3,2,1,0:T(8,128)}, f32[4,128,128]{2,1,0:T(8,128)}), (f32[2,256,128]{1,2,0:T(8,128)}, f32[4,3,3,128,128]{4,3,2,1,0:T(8,128)}, f32[4,128,128]{2,1,0:T(8,128)})) %all-reduce.10.cloned.1.call-update) | async-done | bytes 2883600 | tf_op jit(solution)/shard_map/psum | solution.py:207
  414.1 1.8 copy.14
  415.9 3.4 copy.22
  (260 shorter events, 41.2 us)
Async XLA Ops:
  7.2 44.0 %copy-start.6 = (u32[32]{0:T(128)S(1)}, u32[32]{0:T(128)}, u32[]{:S(2)}) copy-start(u32[32]{0:T(128)} %constant.72) | copy-start | bytes 388
  7.2 44.6 %copy-start.5 = (u32[32]{0:T(128)S(1)}, u32[32]{0:T(128)}, u32[]{:S(2)}) copy-start(u32[32]{0:T(128)} %constant.68) | copy-start | bytes 388
  7.2 39.7 %copy-start.1 = (bf16[4,128,128]{2,1,0:T(8,128)(2,1)S(1)}, bf16[4,128,128]{2,1,0:T(8,128)(2,1)}, u32[]{:S(2)}) copy-start(bf16[4,128,128]{2,1,0:T(8,128)(2,1)} %param.12) | copy-start | bytes 393220
  7.2 291.0 %all-reduce.8.cloned.1.call-start = ((), (), s32[]{:S(2)}) async-start(), calls=%async_computation | async-start | bytes 5767168 | tf_op jit(solution)/shard_map/psum | solution.py:207
  34.6 3.9 collective-permute-start
  35.9 5.5 %collective-permute-start.1 = (bf16[1,8,128]{2,1,0:T(8,128)(2,1)S(1)}, bf16[1,8,128]{2,1,0:T(8,128)(2,1)S(1)}, u32[]{:S(2)}, u32[]{:S(2)}) collective-permute-start(bf16[1,8,128]{2,1,0:T(8,128)(2,1)S(1)} %get-tuple-element.75), channel_id=1, source_target_pairs={{4,0},{8,4},{12,8},{5,1},{9,5},{13,9},{6,2},{10,6},{14,10},{7,3},{... | collective-permute-start | bytes 6152 | tf_op jit(solution)/shard_map/ppermute | solution.py:19
  41.4 2.7 collective-permute-start.2
  42.7 3.1 collective-permute-start.3
  46.7 48.2 %copy-start.3 = (bf16[8,8,128]{2,1,0:T(8,128)(2,1)S(1)}, bf16[8,8,128]{2,1,0:T(8,128)(2,1)}, u32[]{:S(2)}) copy-start(bf16[8,8,128]{2,1,0:T(8,128)(2,1)} %param.13) | copy-start | bytes 49156
  47.4 6.6 %collective-permute-start.4 = (bf16[2,8,128]{2,1,0:T(8,128)(2,1)S(1)}, bf16[2,8,128]{2,1,0:T(8,128)(2,1)S(1)}, u32[]{:S(2)}, u32[]{:S(2)}) collective-permute-start(bf16[2,8,128]{2,1,0:T(8,128)(2,1)S(1)} %get-tuple-element.72), channel_id=1, source_target_pairs={{0,4},{4,8},{8,12},{1,5},{5,9},{9,13},{2,6},{6,10},{10,14},{3,7},{... | collective-permute-start | bytes 12296 | tf_op jit(solution)/shard_map/ppermute | solution.py:18
  49.7 5.5 %collective-permute-start.5 = (bf16[2,8,128]{2,1,0:T(8,128)(2,1)S(1)}, bf16[2,8,128]{2,1,0:T(8,128)(2,1)S(1)}, u32[]{:S(2)}, u32[]{:S(2)}) collective-permute-start(bf16[2,8,128]{2,1,0:T(8,128)(2,1)S(1)} %get-tuple-element.73), channel_id=1, source_target_pairs={{4,0},{8,4},{12,8},{5,1},{9,5},{13,9},{6,2},{10,6},{14,10},{7,3},{... | collective-permute-start | bytes 12296 | tf_op jit(solution)/shard_map/ppermute | solution.py:19
  55.3 4.1 collective-permute-start.6
  57.9 3.8 collective-permute-start.7
  63.3 5.3 %collective-permute-start.8 = (bf16[4,8,128]{2,1,0:T(8,128)(2,1)S(1)}, bf16[4,8,128]{2,1,0:T(8,128)(2,1)S(1)}, u32[]{:S(2)}, u32[]{:S(2)}) collective-permute-start(bf16[4,8,128]{2,1,0:T(8,128)(2,1)S(1)} %get-tuple-element.70), channel_id=1, source_target_pairs={{0,4},{4,8},{8,12},{1,5},{5,9},{9,13},{2,6},{6,10},{10,14},{3,7},{... | collective-permute-start | bytes 24584 | tf_op jit(solution)/shard_map/ppermute | solution.py:18
  67.2 5.5 %collective-permute-start.9 = (bf16[4,8,128]{2,1,0:T(8,128)(2,1)S(1)}, bf16[4,8,128]{2,1,0:T(8,128)(2,1)S(1)}, u32[]{:S(2)}, u32[]{:S(2)}) collective-permute-start(bf16[4,8,128]{2,1,0:T(8,128)(2,1)S(1)} %get-tuple-element.71), channel_id=1, source_target_pairs={{4,0},{8,4},{12,8},{5,1},{9,5},{13,9},{6,2},{10,6},{14,10},{7,3},{... | collective-permute-start | bytes 24584 | tf_op jit(solution)/shard_map/ppermute | solution.py:19
  72.8 7.2 %collective-permute-start.10 = (bf16[16,4,128]{2,1,0:T(4,128)(2,1)S(1)}, bf16[16,4,128]{2,1,0:T(4,128)(2,1)S(1)}, u32[]{:S(2)}, u32[]{:S(2)}) collective-permute-start(bf16[16,4,128]{2,1,0:T(4,128)(2,1)S(1)} %get-tuple-element.46), channel_id=1, source_target_pairs={{0,1},{1,2},{2,3},{4,5},{5,6},{6,7},{8,9},{9,10},{10,11},{12,13},{... | collective-permute-start | bytes 49160 | tf_op jit(solution)/shard_map/ppermute | solution.py:18
  75.6 4.1 collective-permute-start.11
  81.0 6.0 %collective-permute-start.13 = (bf16[8,8,128]{2,1,0:T(8,128)(2,1)S(1)}, bf16[8,8,128]{2,1,0:T(8,128)(2,1)S(1)}, u32[]{:S(2)}, u32[]{:S(2)}) collective-permute-start(bf16[8,8,128]{2,1,0:T(8,128)(2,1)S(1)} %fusion.106), channel_id=1, source_target_pairs={{4,0},{8,4},{12,8},{5,1},{9,5},{13,9},{6,2},{10,6},{14,10},{7,3},{... | collective-permute-start | bytes 49160 | tf_op jit(solution)/shard_map/ppermute | solution.py:19
  82.3 6.0 %collective-permute-start.12 = (bf16[8,8,128]{2,1,0:T(8,128)(2,1)S(1)}, bf16[8,8,128]{2,1,0:T(8,128)(2,1)S(1)}, u32[]{:S(2)}, u32[]{:S(2)}) collective-permute-start(bf16[8,8,128]{2,1,0:T(8,128)(2,1)S(1)} %fusion.106), channel_id=1, source_target_pairs={{0,4},{4,8},{8,12},{1,5},{5,9},{9,13},{2,6},{6,10},{10,14},{3,7},{... | collective-permute-start | bytes 49160 | tf_op jit(solution)/shard_map/ppermute | solution.py:18
  88.3 5.4 %collective-permute-start.15 = (bf16[24,8,128]{2,1,0:T(8,128)(2,1)S(1)}, bf16[24,8,128]{2,1,0:T(8,128)(2,1)S(1)}, u32[]{:S(2)}, u32[]{:S(2)}) collective-permute-start(bf16[24,8,128]{2,1,0:T(8,128)(2,1)S(1)} %pad_maximum_fusion.3), channel_id=1, source_target_pairs={{1,0},{2,1},{3,2},{5,4},{6,5},{7,6},{9,8},{10,9},{11,10},{13,12},{... | collective-permute-start | bytes 147464 | tf_op jit(solution)/shard_map/ppermute | solution.py:19
  89.6 4.7 %collective-permute-start.14 = (bf16[24,8,128]{2,1,0:T(8,128)(2,1)S(1)}, bf16[24,8,128]{2,1,0:T(8,128)(2,1)S(1)}, u32[]{:S(2)}, u32[]{:S(2)}) collective-permute-start(bf16[24,8,128]{2,1,0:T(8,128)(2,1)S(1)} %pad_maximum_fusion.3), channel_id=1, source_target_pairs={{0,1},{1,2},{2,3},{4,5},{5,6},{6,7},{8,9},{9,10},{10,11},{12,13},{... | collective-permute-start | bytes 147464 | tf_op jit(solution)/shard_map/ppermute | solution.py:18
  95.1 8.3 %collective-permute-start.17 = (bf16[8,8,128]{2,1,0:T(8,128)(2,1)S(1)}, bf16[8,8,128]{2,1,0:T(8,128)(2,1)S(1)}, u32[]{:S(2)}, u32[]{:S(2)}) collective-permute-start(bf16[8,8,128]{2,1,0:T(8,128)(2,1)S(1)} %fusion.50), channel_id=1, source_target_pairs={{4,0},{8,4},{12,8},{5,1},{9,5},{13,9},{6,2},{10,6},{14,10},{7,3},{... | collective-permute-start | bytes 49160 | tf_op jit(solution)/shard_map/ppermute | solution.py:19
  96.4 7.0 %collective-permute-start.16 = (bf16[8,8,128]{2,1,0:T(8,128)(2,1)S(1)}, bf16[8,8,128]{2,1,0:T(8,128)(2,1)S(1)}, u32[]{:S(2)}, u32[]{:S(2)}) collective-permute-start(bf16[8,8,128]{2,1,0:T(8,128)(2,1)S(1)} %fusion.50), channel_id=1, source_target_pairs={{0,4},{4,8},{8,12},{1,5},{5,9},{9,13},{2,6},{6,10},{10,14},{3,7},{... | collective-permute-start | bytes 49160 | tf_op jit(solution)/shard_map/ppermute | solution.py:18
  103.4 5.2 %collective-permute-start.19 = (bf16[24,8,128]{2,1,0:T(8,128)(2,1)S(1)}, bf16[24,8,128]{2,1,0:T(8,128)(2,1)S(1)}, u32[]{:S(2)}, u32[]{:S(2)}) collective-permute-start(bf16[24,8,128]{2,1,0:T(8,128)(2,1)S(1)} %pad_maximum_fusion.4), channel_id=1, source_target_pairs={{0,1},{1,2},{2,3},{4,5},{5,6},{6,7},{8,9},{9,10},{10,11},{12,13},{... | collective-permute-start | bytes 147464 | tf_op jit(solution)/shard_map/ppermute | solution.py:18
  107.1 5.3 %collective-permute-start.18 = (bf16[24,8,128]{2,1,0:T(8,128)(2,1)S(1)}, bf16[24,8,128]{2,1,0:T(8,128)(2,1)S(1)}, u32[]{:S(2)}, u32[]{:S(2)}) collective-permute-start(bf16[24,8,128]{2,1,0:T(8,128)(2,1)S(1)} %pad_maximum_fusion.4), channel_id=1, source_target_pairs={{1,0},{2,1},{3,2},{5,4},{6,5},{7,6},{9,8},{10,9},{11,10},{13,12},{... | collective-permute-start | bytes 147464 | tf_op jit(solution)/shard_map/ppermute | solution.py:19
  113.7 7.3 %collective-permute-start.20 = (bf16[4,8,128]{2,1,0:T(8,128)(2,1)S(1)}, bf16[4,8,128]{2,1,0:T(8,128)(2,1)S(1)}, u32[]{:S(2)}, u32[]{:S(2)}) collective-permute-start(bf16[4,8,128]{2,1,0:T(8,128)(2,1)S(1)} %get-tuple-element.68), channel_id=1, source_target_pairs={{0,4},{4,8},{8,12},{1,5},{5,9},{9,13},{2,6},{6,10},{10,14},{3,7},{... | collective-permute-start | bytes 24584 | tf_op jit(solution)/shard_map/ppermute | solution.py:18
  117.7 5.5 %collective-permute-start.21 = (bf16[4,8,128]{2,1,0:T(8,128)(2,1)S(1)}, bf16[4,8,128]{2,1,0:T(8,128)(2,1)S(1)}, u32[]{:S(2)}, u32[]{:S(2)}) collective-permute-start(bf16[4,8,128]{2,1,0:T(8,128)(2,1)S(1)} %get-tuple-element.69), channel_id=1, source_target_pairs={{4,0},{8,4},{12,8},{5,1},{9,5},{13,9},{6,2},{10,6},{14,10},{7,3},{... | collective-permute-start | bytes 24584 | tf_op jit(solution)/shard_map/ppermute | solution.py:19
  123.2 6.3 %collective-permute-start.22 = (bf16[16,4,128]{2,1,0:T(4,128)(2,1)S(1)}, bf16[16,4,128]{2,1,0:T(4,128)(2,1)S(1)}, u32[]{:S(2)}, u32[]{:S(2)}) collective-permute-start(bf16[16,4,128]{2,1,0:T(4,128)(2,1)S(1)} %get-tuple-element.44), channel_id=1, source_target_pairs={{1,0},{2,1},{3,2},{5,4},{6,5},{7,6},{9,8},{10,9},{11,10},{13,12},{... | collective-permute-start | bytes 49160 | tf_op jit(solution)/shard_map/ppermute | solution.py:19
  124.5 4.7 %collective-permute-start.23 = (bf16[16,4,128]{2,1,0:T(4,128)(2,1)S(1)}, bf16[16,4,128]{2,1,0:T(4,128)(2,1)S(1)}, u32[]{:S(2)}, u32[]{:S(2)}) collective-permute-start(bf16[16,4,128]{2,1,0:T(4,128)(2,1)S(1)} %get-tuple-element.45), channel_id=1, source_target_pairs={{0,1},{1,2},{2,3},{4,5},{5,6},{6,7},{8,9},{9,10},{10,11},{12,13},{... | collective-permute-start | bytes 49160 | tf_op jit(solution)/shard_map/ppermute | solution.py:18
  132.1 5.4 %collective-permute-start.24 = (bf16[2,8,128]{2,1,0:T(8,128)(2,1)S(1)}, bf16[2,8,128]{2,1,0:T(8,128)(2,1)S(1)}, u32[]{:S(2)}, u32[]{:S(2)}) collective-permute-start(bf16[2,8,128]{2,1,0:T(8,128)(2,1)S(1)} %get-tuple-element.66), channel_id=1, source_target_pairs={{0,4},{4,8},{8,12},{1,5},{5,9},{9,13},{2,6},{6,10},{10,14},{3,7},{... | collective-permute-start | bytes 12296 | tf_op jit(solution)/shard_map/ppermute | solution.py:18
  135.4 5.5 %collective-permute-start.25 = (bf16[2,8,128]{2,1,0:T(8,128)(2,1)S(1)}, bf16[2,8,128]{2,1,0:T(8,128)(2,1)S(1)}, u32[]{:S(2)}, u32[]{:S(2)}) collective-permute-start(bf16[2,8,128]{2,1,0:T(8,128)(2,1)S(1)} %get-tuple-element.67), channel_id=1, source_target_pairs={{4,0},{8,4},{12,8},{5,1},{9,5},{13,9},{6,2},{10,6},{14,10},{7,3},{... | collective-permute-start | bytes 12296 | tf_op jit(solution)/shard_map/ppermute | solution.py:19
  140.9 4.5 %collective-permute-start.26 = (bf16[12,2,128]{2,1,0:T(2,128)(2,1)S(1)}, bf16[12,2,128]{2,1,0:T(2,128)(2,1)S(1)}, u32[]{:S(2)}, u32[]{:S(2)}) collective-permute-start(bf16[12,2,128]{2,1,0:T(2,128)(2,1)S(1)} %get-tuple-element.50), channel_id=1, source_target_pairs={{1,0},{2,1},{3,2},{5,4},{6,5},{7,6},{9,8},{10,9},{11,10},{13,12},{... | collective-permute-start | bytes 18440 | tf_op jit(solution)/shard_map/ppermute | solution.py:19
  142.2 3.8 collective-permute-start.27
  149.5 7.4 %collective-permute-start.28 = (bf16[1,8,128]{2,1,0:T(8,128)(2,1)S(1)}, bf16[1,8,128]{2,1,0:T(8,128)(2,1)S(1)}, u32[]{:S(2)}, u32[]{:S(2)}) collective-permute-start(bf16[1,8,128]{2,1,0:T(8,128)(2,1)S(1)} %get-tuple-element.64), channel_id=1, source_target_pairs={{0,4},{4,8},{8,12},{1,5},{5,9},{9,13},{2,6},{6,10},{10,14},{3,7},{... | collective-permute-start | bytes 6152 | tf_op jit(solution)/shard_map/ppermute | solution.py:18
  152.8 5.5 %collective-permute-start.29 = (bf16[1,8,128]{2,1,0:T(8,128)(2,1)S(1)}, bf16[1,8,128]{2,1,0:T(8,128)(2,1)S(1)}, u32[]{:S(2)}, u32[]{:S(2)}) collective-permute-start(bf16[1,8,128]{2,1,0:T(8,128)(2,1)S(1)} %get-tuple-element.65), channel_id=1, source_target_pairs={{4,0},{8,4},{12,8},{5,1},{9,5},{13,9},{6,2},{10,6},{14,10},{7,3},{... | collective-permute-start | bytes 6152 | tf_op jit(solution)/shard_map/ppermute | solution.py:19
  154.6 80.4 %copy-start.4 = (bf16[2,256]{1,0:T(2,128)(2,1)S(1)}, bf16[2,256]{1,0:T(2,128)(2,1)}, u32[]{:S(2)}) copy-start(bf16[2,256]{1,0:T(2,128)(2,1)} %param.7) | copy-start | bytes 3076
  158.3 6.1 %collective-permute-start.30 = (bf16[10,1,128]{2,1,0:T(2,128)(2,1)S(1)}, bf16[10,1,128]{2,1,0:T(2,128)(2,1)S(1)}, u32[]{:S(2)}, u32[]{:S(2)}) collective-permute-start(bf16[10,1,128]{2,1,0:T(2,128)(2,1)S(1)} %get-tuple-element.58), channel_id=1, source_target_pairs={{1,0},{2,1},{3,2},{5,4},{6,5},{7,6},{9,8},{10,9},{11,10},{13,12},{... | collective-permute-start | bytes 7688 | tf_op jit(solution)/shard_map/ppermute | solution.py:19
  159.6 5.4 %collective-permute-start.31 = (bf16[10,1,128]{2,1,0:T(2,128)(2,1)S(1)}, bf16[10,1,128]{2,1,0:T(2,128)(2,1)S(1)}, u32[]{:S(2)}, u32[]{:S(2)}) collective-permute-start(bf16[10,1,128]{2,1,0:T(2,128)(2,1)S(1)} %get-tuple-element.59), channel_id=1, source_target_pairs={{0,1},{1,2},{2,3},{4,5},{5,6},{6,7},{8,9},{9,10},{10,11},{12,13},{... | collective-permute-start | bytes 7688 | tf_op jit(solution)/shard_map/ppermute | solution.py:18
  236.2 75.2 %copy-start = (bf16[2,256,128]{2,1,0:T(8,128)(2,1)S(1)}, bf16[2,256,128]{2,1,0:T(8,128)(2,1)}, u32[]{:S(2)}) copy-start(bf16[2,256,128]{2,1,0:T(8,128)(2,1)} %param.9) | copy-start | bytes 393220
  236.2 177.9 %all-reduce.10.cloned.1.call-start = ((), (), s32[]{:S(2)}) async-start(), calls=%async_computation.1 | async-start | bytes 5767168 | tf_op jit(solution)/shard_map/psum | solution.py:207
  415.9 3.4 copy-start.2
Sparse Core Ops, SparseCore 0:
  236.3 61.8 all-reduce.7
  300.8 113.3 all-reduce.9
